TPU v7x, 256 devices: a whole 4x4x8 slice. The times are simulated.
256 devices in a mesh: seq: 32 (over z, y), exp: 8 (over x, core).
Axes of the slice: x: 4, y: 4, z: 8, core: 2. Of those that a mesh axis runs over, the one named last changes fastest.
Arguments:
- resid_rows: bfloat16 [8, 128, 3072], P('exp', 'seq'), may hold values from -6 to 6
- query_rows: bfloat16 [8, 128, 3072], P('exp', 'seq'), may hold values from -6 to 6
- key_rows: bfloat16 [8, 4096, 3072], P('exp', 'seq'), may hold values from -6 to 6
- value_rows: bfloat16 [8, 4096, 3072], P('exp', 'seq'), may hold values from -6 to 6
- log_decay: float32 [8, 48, 4096], P('exp', None, 'seq'), may hold values from -1 to 0
- read_pos: int32 [8, 128], P('exp', 'seq'), may hold values from 0 to 4095, as said below
- expert_ids: int32 [8, 128, 2], P('exp', 'seq'), may hold values from 0 to 7, all different within a row; in each aligned block of 4 rows (0 to 3, 4 to 7, ..., all dimensions but the last counted through in order) at most 2 rows name the same one
- pair_order: int32 [8], replicated, may hold values from 0 to 7, each once
- lengths: int32 [8], replicated, may hold values from 1 to 4096
- norm_gain: bfloat16 [3072], replicated, may hold values from 0.5 to 1.5
- router_weight: bfloat16 [3072, 8], replicated, may hold values from -0.109375 to 0.109375
- score_weight: bfloat16 [3072], replicated, may hold values from -0.109375 to 0.109375
- gate_weight: bfloat16 [8, 3072, 9216], P('exp', None, 'seq'), may hold values from -0.109375 to 0.109375
- up_weight: bfloat16 [8, 3072, 9216], P('exp', None, 'seq'), may hold values from -0.109375 to 0.109375
- down_weight: bfloat16 [8, 9216, 3072], P('exp', 'seq'), may hold values from -0.0625 to 0.0625
Outputs:
- pair_loss: float32 [], replicated
- grad_query: float32 [8, 128, 3072], P('exp', 'seq')
- grad_resid: float32 [8, 128, 3072], P('exp', 'seq')
- grad_keys: bfloat16 [8, 4096, 3072], P('exp', 'seq')
- grad_values: bfloat16 [8, 4096, 3072], P('exp', 'seq')
Inputs may be any that keep to these rules, and one draw needn't show every extreme that they name: `read_pos`: each aligned block j of 4 entries of a sequence holds strictly increasing positions from j * 128 to (j + 1) * 128 - 1, the last of them being (j + 1) * 128 - 1. `expert_ids`: the two entries of a row differ; in the rows of one device (aligned blocks of 4 rows) no expert is named by more than 2 rows. `pair_order`: each sequence appears once.
All inputs are finite; a program needn't handle non-finite values.
Results may differ from a plain program's by a relative error of at most 0.018.
Values may be sent and summed in bfloat16 or wider, within the bound.
No kernel may reach another device: no remote copies, remote signals or barrier semaphores. Data moves between devices by JAX's collectives and lax.ppermute only.
A program may use at most 128 MiB of HBM per device.

v0:
```python
import jax
import jax.numpy as jnp
from jax import lax
from jax.sharding import PartitionSpec as P

PRECISE = lax.Precision.HIGHEST
EPSILON = 1e-06
LENGTH_WEIGHT = 4.0
SCORE_SCALE = 256.0


def carried_in(value, axis, join, neutral, backward):
    count = lax.axis_size(axis)
    place = lax.axis_index(axis)
    ahead = count - 1 - place if backward else place
    gathered = jax.tree.map(
        lambda a, kind: lax.all_gather(a.astype(kind), axis), value, (jnp.bfloat16, jnp.bfloat16)
    )
    state = jax.tree.map(lambda a, e: jnp.zeros_like(a) + jnp.asarray(e, a.dtype), value, neutral)

    def one(lap, state):
        source = count - 1 - lap if backward else lap
        return join(
            state,
            jax.tree.map(
                lambda a, own: lax.dynamic_index_in_dim(a, source, 0, False).astype(own.dtype),
                gathered,
                value,
            ),
        )

    return lax.fori_loop(0, ahead, one, state)


def merge_states(earlier, later):
    return (earlier[0] * later[0], later[0][:, None, None] * earlier[1] + later[1])


def chain_prefix(decay, summary, backwards):
    blank = (jnp.ones_like(decay), jnp.zeros_like(summary))
    joined = carried_in((decay, summary), "seq", merge_states, blank, backwards)
    return joined[1]


def readout_weights(cumulated, places):
    positions = jnp.arange(cumulated.shape[1], dtype=jnp.int32)
    one_hot = (places[:, None] == positions[None, :]).astype(jnp.float32)
    at_read = jnp.dot(cumulated, one_hot.T, precision=PRECISE)
    allowed = positions[None, :] <= places[:, None]
    exponent = jnp.where(allowed[None], at_read[:, :, None] - cumulated[:, None, :], -1e30)
    return (at_read, jnp.exp(exponent))


def preference_loss(rewards, pair_order, lengths, total_length):
    count = rewards.shape[0]
    ordering = (pair_order[:, None] == jnp.arange(count, dtype=jnp.int32)[None, :]).astype(
        jnp.float32
    )
    ranked = jnp.dot(ordering, rewards, precision=PRECISE).reshape(count // 2, 2)
    fitted = jnp.mean(jax.nn.softplus(ranked[:, 1] - ranked[:, 0]))
    share = lengths.astype(jnp.float32) / total_length
    scatter_breadth = jnp.mean((rewards - jnp.mean(rewards)) * (share - jnp.mean(share)))
    return fitted + LENGTH_WEIGHT * scatter_breadth * scatter_breadth


def to_experts(slots):
    return lax.all_to_all(slots, "exp", split_axis=0, concat_axis=0, tiled=True)


def over_slots(arrived, project):
    return project(lax.all_gather(arrived, "seq", axis=0, tiled=True), jnp.int32(0))


def collect(project, expert_count, capacity):
    slot_count = expert_count * capacity
    summed = lax.psum_scatter(
        project(jnp.int32(0), slot_count * lax.axis_size("seq")).astype(jnp.bfloat16),
        "seq",
        scatter_dimension=0,
        tiled=True,
    )
    shaped = summed.reshape(expert_count, capacity, -1)
    return lax.all_to_all(shaped, "exp", split_axis=0, concat_axis=0, tiled=True)


def per_device(
    resid_rows,
    query_rows,
    key_rows,
    value_rows,
    log_decay,
    read_pos,
    expert_ids,
    pair_order,
    lengths,
    norm_gain,
    router_weight,
    score_weight,
    gate_weight,
    up_weight,
    down_weight,
):
    seq_count = lax.axis_size("seq")
    exp_count = lax.axis_size("exp")
    seq_index = lax.axis_index("seq")
    exp_index = lax.axis_index("exp")
    token_count = key_rows.shape[1]
    model_width = key_rows.shape[2]
    head_count = log_decay.shape[1]
    head_size = model_width // head_count
    read_count = query_rows.shape[1]
    expert_count = router_weight.shape[1]
    capacity = max(2, 4 * read_count // exp_count)
    keys_half = key_rows[0].reshape(token_count, head_count, head_size)
    values_half = value_rows[0].reshape(token_count, head_count, head_size)
    query_half = query_rows[0].reshape(read_count, head_count, head_size)
    keys_float = keys_half.astype(jnp.float32)
    values_float = values_half.astype(jnp.float32)
    query_float = query_half.astype(jnp.float32)
    cumulated = jnp.cumsum(log_decay[0], axis=1)
    group_decay = jnp.exp(cumulated[:, -1])
    tail_decay = jnp.exp(cumulated[:, -1:] - cumulated).T[:, :, None]
    own_state = jnp.einsum("thi,thj->hij", keys_float * tail_decay, values_float, precision=PRECISE)
    state_in = chain_prefix(group_decay, own_state, False)
    places = read_pos[0] - seq_index * token_count
    at_read, weight = readout_weights(cumulated, places)
    lift = jnp.exp(at_read).T[:, :, None]
    query_key = (
        jnp.einsum("rhi,thi->hrt", query_half, keys_half, preferred_element_type=jnp.float32)
        / head_size
    )
    attended = jnp.einsum("hrt,thj->rhj", weight * query_key, values_float, precision=PRECISE)
    attended = (
        attended
        + lift * jnp.einsum("rhi,hij->rhj", query_float, state_in, precision=PRECISE) / head_size
    )
    residual = resid_rows[0].astype(jnp.float32) + attended.reshape(read_count, model_width)
    inverse = lax.rsqrt(jnp.mean(residual * residual, axis=1, keepdims=True) + EPSILON)
    unit_rows = residual * inverse
    gain_float = norm_gain.astype(jnp.float32)
    normed = (unit_rows * gain_float).astype(jnp.bfloat16)
    logits = jnp.dot(normed, router_weight, preferred_element_type=jnp.float32)
    picks = (
        expert_ids[0][:, :, None] == jnp.arange(expert_count, dtype=jnp.int32)[None, None, :]
    ).astype(jnp.float32)
    chosen = jnp.einsum("rke,re->rk", picks, logits, precision=PRECISE)
    first = jax.nn.sigmoid(chosen[:, 0] - chosen[:, 1])
    gates = jnp.stack([first, 1.0 - first], axis=1)
    flat = picks.reshape(read_count * 2, expert_count)
    earlier = jnp.cumsum(flat, axis=0) - flat
    slot_index = jnp.sum(earlier * flat, axis=1)
    slot_hot = (slot_index[:, None] == jnp.arange(capacity, dtype=jnp.float32)[None, :]).astype(
        jnp.float32
    )
    placement = (
        (flat[:, :, None] * slot_hot[:, None, :])
        .reshape(read_count * 2, expert_count * capacity)
        .astype(jnp.bfloat16)
    )
    doubled = jnp.repeat(normed, 2, axis=0)
    outgoing = jnp.dot(placement.T, doubled, preferred_element_type=jnp.float32).astype(
        jnp.bfloat16
    )
    arrived = to_experts(outgoing.reshape(expert_count, capacity, model_width)).reshape(
        expert_count * capacity, model_width
    )
    gate_w = gate_weight[0]
    up_w = up_weight[0]
    down_w = down_weight[0]
    hidden_count = gate_w.shape[1]

    def project_in(piece, start):
        gate_part = jnp.dot(piece, gate_w, preferred_element_type=jnp.float32)
        up_part = jnp.dot(piece, up_w, preferred_element_type=jnp.float32)
        return jnp.concatenate([gate_part, up_part], axis=1)

    projected = over_slots(arrived, project_in)
    pre_gate = projected[:, :hidden_count]
    pre_up = projected[:, hidden_count:]
    gate_sigmoid = jax.nn.sigmoid(pre_gate)
    activated = (pre_gate * gate_sigmoid * pre_up).astype(jnp.bfloat16)

    def project_out(start, count):
        return jnp.dot(activated, down_w, preferred_element_type=jnp.float32)

    returned = collect(project_out, expert_count, capacity)
    expert_out = jnp.dot(
        placement,
        returned.reshape(expert_count * capacity, model_width),
        preferred_element_type=jnp.float32,
    )
    expert_out = expert_out.reshape(read_count, 2, model_width)
    mixed = residual + jnp.sum(gates[:, :, None] * expert_out, axis=1)
    score_float = score_weight.astype(jnp.float32)
    score = jnp.dot(mixed, score_float, precision=PRECISE)
    own_total = jnp.sum(score) / (read_count * seq_count)
    marked = jnp.where(jnp.arange(exp_count) == exp_index, own_total, 0.0)
    rewards = lax.psum(marked, ("seq", "exp"))
    pair_loss, d_reward = jax.value_and_grad(preference_loss)(
        rewards, pair_order, lengths, token_count * seq_count
    )
    own_grad = jnp.sum(jnp.where(jnp.arange(exp_count) == exp_index, d_reward, 0.0)) * SCORE_SCALE
    d_mixed = jnp.broadcast_to((own_grad * score_float)[None, :], (read_count, model_width))
    d_out = (gates[:, :, None] * d_mixed[:, None, :]).astype(jnp.bfloat16)
    d_gates = jnp.einsum("rd,rkd->rk", d_mixed, expert_out, precision=PRECISE)
    d_logit = (d_gates[:, 0] - d_gates[:, 1]) * first * (1.0 - first)
    back_out = jnp.dot(
        placement.T, d_out.reshape(read_count * 2, model_width), preferred_element_type=jnp.float32
    ).astype(jnp.bfloat16)
    back_arrived = to_experts(back_out.reshape(expert_count, capacity, model_width)).reshape(
        expert_count * capacity, model_width
    )

    def project_back(piece, start):
        return jnp.einsum("sd,fd->sf", piece, down_w, preferred_element_type=jnp.float32)

    d_act = over_slots(back_arrived, project_back)
    d_pre_gate = (d_act * pre_up * gate_sigmoid * (1.0 + pre_gate * (1.0 - gate_sigmoid))).astype(
        jnp.bfloat16
    )
    d_pre_up = (d_act * pre_gate * gate_sigmoid).astype(jnp.bfloat16)

    def project_in_back(start, count):
        gate_term = jnp.einsum("sf,df->sd", d_pre_gate, gate_w, preferred_element_type=jnp.float32)
        up_term = jnp.einsum("sf,df->sd", d_pre_up, up_w, preferred_element_type=jnp.float32)
        return gate_term + up_term

    d_in_slots = collect(project_in_back, expert_count, capacity)
    d_in = jnp.dot(
        placement,
        d_in_slots.reshape(expert_count * capacity, model_width),
        preferred_element_type=jnp.float32,
    )
    d_in = d_in.reshape(read_count, 2, model_width)
    columns = jnp.einsum("rke,de->rkd", picks, router_weight.astype(jnp.float32), precision=PRECISE)
    d_normed = jnp.sum(d_in, axis=1) + d_logit[:, None] * (columns[:, 0] - columns[:, 1])
    d_unit = d_normed * gain_float
    grad_resid = d_mixed + inverse * (
        d_unit - unit_rows * jnp.mean(d_unit * unit_rows, axis=1, keepdims=True)
    )
    rounded = grad_resid.astype(jnp.bfloat16)
    d_half = rounded.reshape(read_count, head_count, head_size)
    d_attended = d_half.astype(jnp.float32)
    summary = (
        jnp.einsum("rhi,rhj->hij", query_float * lift, d_attended, precision=PRECISE) / head_size
    )
    suffix = chain_prefix(group_decay, summary, True)
    grad_dot = (
        jnp.einsum("rhj,thj->hrt", d_half, values_half, preferred_element_type=jnp.float32)
        / head_size
    )
    grad_query = jnp.einsum("hrt,thi->rhi", weight * grad_dot, keys_float, precision=PRECISE)
    grad_query = (
        grad_query
        + lift * jnp.einsum("rhj,hij->rhi", d_attended, state_in, precision=PRECISE) / head_size
    )
    grad_keys = jnp.einsum("hrt,rhi->thi", weight * grad_dot, query_float, precision=PRECISE)
    grad_keys = grad_keys + tail_decay * jnp.einsum(
        "hij,thj->thi", suffix, values_float, precision=PRECISE
    )
    grad_values = jnp.einsum("hrt,rhj->thj", weight * query_key, d_attended, precision=PRECISE)
    grad_values = grad_values + tail_decay * jnp.einsum(
        "thi,hij->thj", keys_float, suffix, precision=PRECISE
    )
    return (
        pair_loss,
        grad_query.reshape(1, read_count, model_width),
        grad_resid.reshape(1, read_count, model_width),
        grad_keys.reshape(1, token_count, model_width).astype(jnp.bfloat16),
        grad_values.reshape(1, token_count, model_width).astype(jnp.bfloat16),
    )


def solution(mesh):
    in_specs = (
        P("exp", "seq", None),
        P("exp", "seq", None),
        P("exp", "seq", None),
        P("exp", "seq", None),
        P("exp", None, "seq"),
        P("exp", "seq"),
        P("exp", "seq", None),
        P(),
        P(),
        P(),
        P(),
        P(),
        P("exp", None, "seq"),
        P("exp", None, "seq"),
        P("exp", "seq", None),
    )
    out_specs = (
        P(),
        P("exp", "seq", None),
        P("exp", "seq", None),
        P("exp", "seq", None),
        P("exp", "seq", None),
    )
    return jax.shard_map(
        per_device, mesh=mesh, in_specs=in_specs, out_specs=out_specs, check_vma=False
    )
```

profile of v0, /device:TPU:1, one launch (start us, length us, event | category | flops | bytes accessed | tf_op | source)
XLA Modules:
  0.0 1303.2 jit_solution(8809889284805440682)
XLA Ops:
  12.1 2.2 fusion.17
  16.3 65.9 %all-reduce.2 = bf16[1536]{0:T(1024)(128)(2,1)S(1)} all-reduce(bf16[1536]{0:T(1024)(128)(2,1)S(1)} %dynamic-update-slice), channel_id=2, replica_groups=mesh['seq'=32,'exp'=8] {'seq'}, use_global_device_ids=true, to_apply=%add.2 | all-reduce | flops 1536 | bytes 6144
  89.4 111.9 %all-gather.12.cloned.1.call-done = bf16[1536,64,64]{2,1,0:T(8,128)(2,1)} async-done(((bf16[48,64,64]{2,1,0:T(8,128)(2,1)}), bf16[1536,64,64]{2,1,0:T(8,128)(2,1)}) %all-gather.12.cloned.1.call-update) | async-done | bytes 12582928 | tf_op jit(solution)/shard_map/all_gather | solution.py:17
  212.8 10.7 all_to_all.20
  225.1 137.3 %all-gather.8.cloned.1.call-done = bf16[512,3072]{1,0:T(8,128)(2,1)} async-done(((bf16[16,3072]{1,0:T(8,128)(2,1)}), bf16[512,3072]{1,0:T(8,128)(2,1)}) %all-gather.8.cloned.1.call-update) | async-done | bytes 3145744 | tf_op jit(solution)/shard_map/all_gather | solution.py:71
  362.4 3.7 fusion.8
  368.3 3.5 convolution_convert_fusion
  382.1 207.1 %reduce-scatter.3.cloned.1.call-done = bf16[16,3072]{1,0:T(8,128)(2,1)} async-done(((bf16[512,3072]{1,0:T(8,128)(2,1)}), bf16[16,3072]{1,0:T(8,128)(2,1)}) %reduce-scatter.3.cloned.1.call-update) | async-done | bytes 98320 | tf_op jit(solution)/shard_map/reduce_scatter | solution.py:76
  590.8 10.0 all-to-all-start.1
  603.3 2.6 all-to-all-done.1
  613.3 74.1 %psum.7 = f32[8]{0:T(128)} all-reduce(f32[8]{0:T(128)} %compare_select_fusion.4), channel_id=1, replica_groups=mesh['seq'=32,'exp'=8] {'seq','exp'}, use_global_device_ids=true, to_apply=%region_9.10 | all-reduce | flops 8 | bytes 64 | tf_op jit(solution)/shard_map/psum | solution.py:198
  705.9 9.6 all_to_all.21
  717.2 72.2 %all-gather.10.cloned.1.call-done = bf16[512,3072]{1,0:T(8,128)(2,1)} async-done(((bf16[16,3072]{1,0:T(8,128)(2,1)}), bf16[512,3072]{1,0:T(8,128)(2,1)}) %all-gather.10.cloned.1.call-update) | async-done | bytes 3145744 | tf_op jit(solution)/shard_map/all_gather | solution.py:71
  789.4 3.1 fusion
  794.7 3.7 add_convert_fusion
  800.2 215.3 %reduce-scatter.5.cloned.1.call-done = bf16[16,3072]{1,0:T(8,128)(2,1)} async-done(((bf16[512,3072]{1,0:T(8,128)(2,1)}), bf16[16,3072]{1,0:T(8,128)(2,1)}) %reduce-scatter.5.cloned.1.call-update) | async-done | bytes 98320 | tf_op jit(solution)/shard_map/reduce_scatter | solution.py:76
  1017.2 10.0 all-to-all-start.3
  1027.3 4.9 all-to-all-done.3
  1033.6 3.2 multiply_convert_fusion
  1049.3 167.0 %all-gather.14.cloned.1.call-done = bf16[1536,64,64]{2,1,0:T(8,128)(2,1)} async-done(((bf16[48,64,64]{2,1,0:T(8,128)(2,1)}), bf16[1536,64,64]{2,1,0:T(8,128)(2,1)}) %all-gather.14.cloned.1.call-update) | async-done | bytes 12582928 | tf_op jit(solution)/shard_map/all_gather | solution.py:17
  1216.5 68.8 %while.27 = (s32[]{:T(128)}, f32[48,64,64]{2,1,0:T(8,128)S(1)}, s32[]{:T(128)}, bf16[32,48]{1,0:T(8,128)(2,1)}, bf16[32,48,64,64]{3,2,1,0:T(8,128)(2,1)}, /*index=5*/s32[]{:T(128)}, s32[]{:T(128)}, s32[]{:T(128)}, s32[]{:T(128)}) while((s32[]{:T(128)}, f32[48,64,64]{2,1,0:T(8,128)S(1)}, s32[]{:T(128)}, bf16[32,48]{1,0:T(8,128)(2,1)}, ...), condition=%wide.region_20.21_spmd, body=%wide.region_19.20_spmd.sunk | while | flops 589878 | bytes 1966715 | solution.py:32
  1285.3 2.4 fusion.13
  1288.9 4.1 fusion.11
  1293.0 2.3 copy.78
  (278 shorter events, 152.6 us)
Async XLA Ops:
  7.2 361.1 %copy-start = (bf16[1,288,3072]{2,1,0:T(8,128)(2,1)S(1)}, bf16[1,288,3072]{2,1,0:T(8,128)(2,1)}, u32[]{:S(2)}) copy-start(bf16[1,288,3072]{2,1,0:T(8,128)(2,1)} %param.33) | copy-start | bytes 5308420
  7.2 194.1 %all-gather.12.cloned.1.call-start = ((), (), s32[]{:S(2)}) async-start(), calls=%async_computation.10 | async-start | bytes 25952256 | tf_op jit(solution)/shard_map/all_gather | solution.py:17
  8.4 77.3 %copy-start.24 = (f32[48,128]{1,0:T(8,128)}, f32[48,128]{1,0:T(8,128)S(1)}, u32[]{:S(2)}) copy-start(f32[48,128]{1,0:T(8,128)S(1)} %reduce_window_sum.22) | copy-start | bytes 73732
  10.2 75.5 %copy-start.2 = (bf16[1,128,3072]{1,2,0:T(8,128)(2,1)}, bf16[1,128,3072]{1,2,0:T(8,128)(2,1)S(1)}, u32[]{:S(2)}) copy-start(bf16[1,128,3072]{1,2,0:T(8,128)(2,1)S(1)} %copy.58) | copy-start | bytes 2359300
  12.0 74.8 %copy-start.4 = (bf16[1,128,3072]{1,2,0:T(8,128)(2,1)}, bf16[1,128,3072]{1,2,0:T(8,128)(2,1)S(1)}, u32[]{:S(2)}) copy-start(bf16[1,128,3072]{1,2,0:T(8,128)(2,1)S(1)} %copy.60) | copy-start | bytes 2359300
  12.0 70.9 %copy-start.49 = (s32[1,4]{1,0:T(1,128)S(1)}, s32[1,4]{1,0:T(1,128)}, u32[]{:S(2)}) copy-start(s32[1,4]{1,0:T(1,128)} %param.24) | copy-start | bytes 52
  12.1 72.5 %copy-start.36 = (bf16[1,4,3072]{2,1,0:T(4,128)(2,1)S(1)}, bf16[1,4,3072]{2,1,0:T(4,128)(2,1)}, u32[]{:S(2)}) copy-start(bf16[1,4,3072]{2,1,0:T(4,128)(2,1)} %param.20) | copy-start | bytes 73732
  12.1 72.6 %copy-start.25 = (bf16[1,4,3072]{2,1,0:T(4,128)(2,1)S(1)}, bf16[1,4,3072]{2,1,0:T(4,128)(2,1)}, u32[]{:S(2)}) copy-start(bf16[1,4,3072]{2,1,0:T(4,128)(2,1)} %param.19) | copy-start | bytes 73732
  14.3 348.1 %all-gather.8.cloned.1.call-start = ((), (), s32[]{:S(2)}) async-start(), calls=%async_computation.6 | async-start | bytes 3244032 | tf_op jit(solution)/shard_map/all_gather | solution.py:71
  84.6 116.8 %copy-start.12 = (bf16[4,48,64]{2,1,0:T(8,128)(2,1)}, bf16[4,48,64]{2,1,0:T(8,128)(2,1)S(1)}, u32[]{:S(2)}) copy-start(bf16[4,48,64]{2,1,0:T(8,128)(2,1)S(1)} %reshape_squeeze.9) | copy-start | bytes 73732
  85.7 115.8 %copy-start.52 = (pred[4,128]{1,0:T(4,128)(4,1)}, pred[4,128]{1,0:T(4,128)(4,1)S(1)}, u32[]{:S(2)}) copy-start(pred[4,128]{1,0:T(4,128)(4,1)S(1)} %iota_compare_fusion.6) | copy-start | bytes 1540
  225.1 364.1 %reduce-scatter.3.cloned.1.call-start = ((), (), s32[]{:S(2)}) async-start(), calls=%async_computation.7 | async-start | bytes 3244032 | tf_op jit(solution)/shard_map/reduce_scatter | solution.py:76
  590.8 15.1 %all-to-all-start.1 = ((bf16[8,2,3072]{2,1,0:T(2,128)(2,1)}), bf16[8,2,3072]{2,1,0:T(2,128)(2,1)}, u32[]{:S(2)}, u32[]{:S(2)}) async-start(bf16[8,2,3072]{2,1,0:T(2,128)(2,1)} %reshape.392), calls=%async_computation.2 | async-start | bytes 196608 | tf_op jit(solution)/shard_map/all_to_all | solution.py:83
  600.8 188.6 %all-gather.10.cloned.1.call-start = ((), (), s32[]{:S(2)}) async-start(), calls=%async_computation.8 | async-start | bytes 3244032 | tf_op jit(solution)/shard_map/all_gather | solution.py:71
  717.1 298.5 %reduce-scatter.5.cloned.1.call-start = ((), (), s32[]{:S(2)}) async-start(), calls=%async_computation.9 | async-start | bytes 3244032 | tf_op jit(solution)/shard_map/reduce_scatter | solution.py:76
  798.3 228.8 %copy-start.45 = (f32[4,1]{0,1:T(1,128)S(1)}, f32[4,1]{0,1:T(1,128)}, u32[]{:S(2)}) copy-start(f32[4,1]{0,1:T(1,128)} %get-tuple-element.175) | copy-start | bytes 52
  798.4 233.9 %copy-start.39 = (bf16[4,2,16]{2,0,1:T(4,128)(2,1)S(1)}, bf16[4,2,16]{2,0,1:T(4,128)(2,1)}, u32[]{:S(2)}) copy-start(bf16[4,2,16]{2,0,1:T(4,128)(2,1)} %copy.67) | copy-start | bytes 772
  798.4 234.1 %copy-start.18 = (f32[4,3072]{1,0:T(4,128)S(1)}, f32[4,3072]{1,0:T(4,128)}, u32[]{:S(2)}) copy-start(f32[4,3072]{1,0:T(4,128)} %reshape.388) | copy-start | bytes 147460
  798.4 234.1 %copy-start.26 = (bf16[1,4,3072]{2,1,0:T(4,128)(2,1)S(1)}, bf16[1,4,3072]{2,1,0:T(4,128)(2,1)}, u32[]{:S(2)}) copy-start(bf16[1,4,3072]{2,1,0:T(4,128)(2,1)} %param.19) | copy-start | bytes 73732
  798.4 234.1 %copy-start.42 = (f32[4]{0:T(128)S(1)}, f32[4]{0:T(128)}, u32[]{:S(2)}) copy-start(f32[4]{0:T(128)} %add_rsqrt_fusion) | copy-start | bytes 52
  799.0 234.5 %copy-start.13 = (bf16[4,48,64]{2,1,0:T(8,128)(2,1)S(1)}, bf16[4,48,64]{2,1,0:T(8,128)(2,1)}, u32[]{:S(2)}) copy-start(bf16[4,48,64]{2,1,0:T(8,128)(2,1)} %copy-done.12) | copy-start | bytes 73732
  1017.2 15.0 %all-to-all-start.3 = ((bf16[8,2,3072]{2,1,0:T(2,128)(2,1)}), bf16[8,2,3072]{2,1,0:T(2,128)(2,1)S(1)}, u32[]{:S(2)}, u32[]{:S(2)}) async-start(bf16[8,2,3072]{2,1,0:T(2,128)(2,1)} %reshape.398), calls=%async_computation.5 | async-start | bytes 196608 | tf_op jit(solution)/shard_map/all_to_all | solution.py:83
  1027.2 189.1 %all-gather.14.cloned.1.call-start = ((), (), s32[]{:S(2)}) async-start(), calls=%async_computation.11 | async-start | bytes 25952256 | tf_op jit(solution)/shard_map/all_gather | solution.py:17
  1216.5 68.8 %copy-start.22 = (f32[128,48]{0,1:T(8,128)S(1)}, f32[128,48]{0,1:T(8,128)}, u32[]{:S(2)}) copy-start(f32[128,48]{0,1:T(8,128)} %copy-done.21) | copy-start | bytes 73732
  (37 other events, 111.9 us)
Sparse Core Ops, SparseCore 0:
  14.5 186.7 all-gather.11
  225.2 137.1 all-gather.7
  371.9 217.2 reduce-scatter.2
  717.3 72.1 all-gather.9
  798.5 216.9 reduce-scatter.4
  1036.9 179.3 all-gather.13
where the time goes:
time: 1310 us; the launch traced here: 1300 us
  waiting for transfers between devices  918 us (70%)
  blocking collectives  160 us (12%)
  other arithmetic  85.5 us (7%)
  matrix products  54 us (4%)
  local copies, waits for them, and re-layouts  41.1 us (3%)
  between operations  22.6 us (2%)
  starting transfers between devices  20.2 us (2%)
    reduce_scatter x2, waiting for transfers between devices, collect(): lax.psum_scatter(project(jnp.int32(0), slot_count * lax.axis_size('seq'))...  422 us
    all_gather x2, waiting for transfers between devices, carried_in(): lax.all_gather(a.astype(kind), axis)  279 us
    all_gather x2, waiting for transfers between devices, over_slots(): lax.all_gather(arrived, 'seq', axis=0, tiled=True)  210 us
    psum x1, blocking collectives, per_device(): rewards = lax.psum(marked, ('seq', 'exp'))  74.1 us
    unnamed x1, blocking collectives  65.9 us
    add x31, other arithmetic, merge_states(): later[0][:, None, None] * earlier[1] + later[1]  46.5 us
  transfers between devices with their start and end apart: 8, of which 8 were waited for; matrix products, arithmetic and copies ran while one was open for 2% of the time, Pallas kernels for 0%

commit v1 on v0

--- a/solution.py
+++ b/solution.py
@@ -195,7 +195,7 @@
     score = jnp.dot(mixed, score_float, precision=PRECISE)
     own_total = jnp.sum(score) / (read_count * seq_count)
     marked = jnp.where(jnp.arange(exp_count) == exp_index, own_total, 0.0)
-    rewards = lax.psum(marked, ("seq", "exp"))
+    rewards = jax.lax.psum(jax.lax.psum(marked, "seq"), "exp")
     pair_loss, d_reward = jax.value_and_grad(preference_loss)(
         rewards, pair_order, lengths, token_count * seq_count
     )

time: 1310 us -> 1320 us (level)
    psum x1 -> x2, blocking collectives: 74.1 us -> 85.9 us  [per_device(): rewards = jax.lax.psum(jax.lax.psum(marked, 'seq'), 'exp')]
where the time goes in v1:
time: 1320 us
  waiting for transfers between devices  919 us (70%)
  blocking collectives  172 us (13%)
  other arithmetic  85.9 us (7%)
  matrix products  54.1 us (4%)
  local copies, waits for them, and re-layouts  41.5 us (3%)
  between operations  22.9 us (2%)
  starting transfers between devices  20.2 us (2%)
    reduce_scatter x2, waiting for transfers between devices, collect(): lax.psum_scatter(project(jnp.int32(0), slot_count * lax.axis_size('seq'))...  423 us
    all_gather x2, waiting for transfers between devices, carried_in(): lax.all_gather(a.astype(kind), axis)  279 us
    all_gather x2, waiting for transfers between devices, over_slots(): lax.all_gather(arrived, 'seq', axis=0, tiled=True)  209 us
    psum x2, blocking collectives, per_device(): rewards = jax.lax.psum(jax.lax.psum(marked, 'seq'), 'exp')  85.9 us
    unnamed x1, blocking collectives  65.9 us
    add x31, other arithmetic, merge_states(): later[0][:, None, None] * earlier[1] + later[1]  46.5 us
  transfers between devices with their start and end apart: 8, of which 8 were waited for; matrix products, arithmetic and copies ran while one was open for 2% of the time, Pallas kernels for 0%

profile of v1, /device:TPU:1, one launch (start us, length us, event | category | flops | bytes accessed | tf_op | source)
XLA Modules:
  0.0 1316.6 jit_solution(13590087046404356695)
XLA Ops:
  16.3 65.9 %all-reduce.2 = bf16[1536]{0:T(1024)(128)(2,1)S(1)} all-reduce(bf16[1536]{0:T(1024)(128)(2,1)S(1)} %dynamic-update-slice), channel_id=2, replica_groups=mesh['seq'=32,'exp'=8] {'seq'}, use_global_device_ids=true, to_apply=%add.2 | all-reduce | flops 1536 | bytes 6144
  89.4 111.9 %all-gather.12.cloned.1.call-done = bf16[1536,64,64]{2,1,0:T(8,128)(2,1)} async-done(((bf16[48,64,64]{2,1,0:T(8,128)(2,1)}), bf16[1536,64,64]{2,1,0:T(8,128)(2,1)}) %all-gather.12.cloned.1.call-update) | async-done | bytes 12582928 | tf_op jit(solution)/shard_map/all_gather | solution.py:17
  212.9 10.7 all_to_all.20
  225.2 137.3 %all-gather.8.cloned.1.call-done = bf16[512,3072]{1,0:T(8,128)(2,1)} async-done(((bf16[16,3072]{1,0:T(8,128)(2,1)}), bf16[512,3072]{1,0:T(8,128)(2,1)}) %all-gather.8.cloned.1.call-update) | async-done | bytes 3145744 | tf_op jit(solution)/shard_map/all_gather | solution.py:71
  362.5 3.7 fusion.8
  368.4 3.6 convolution_convert_fusion
  382.5 207.0 %reduce-scatter.3.cloned.1.call-done = bf16[16,3072]{1,0:T(8,128)(2,1)} async-done(((bf16[512,3072]{1,0:T(8,128)(2,1)}), bf16[16,3072]{1,0:T(8,128)(2,1)}) %reduce-scatter.3.cloned.1.call-update) | async-done | bytes 98320 | tf_op jit(solution)/shard_map/reduce_scatter | solution.py:76
  591.1 9.7 all-to-all-start.1
  602.1 3.8 all-to-all-done.1
  613.3 58.7 %psum.14 = f32[8]{0:T(128)} all-reduce(f32[8]{0:T(128)} %compare_select_fusion.4), channel_id=1, replica_groups=mesh['seq'=32,'exp'=8] {'seq'}, use_global_device_ids=true, to_apply=%region_9.10 | all-reduce | flops 8 | bytes 64 | tf_op jit(solution)/shard_map/psum | solution.py:198
  673.3 27.2 %psum.15 = f32[8]{0:T(128)} all-reduce(f32[8]{0:T(128)} %psum.14), channel_id=1, replica_groups=mesh['seq'=32,'exp'=8] {'exp'}, use_global_device_ids=true, to_apply=%region_10.11 | all-reduce | flops 8 | bytes 64 | tf_op jit(solution)/shard_map/psum | solution.py:198
  719.7 9.6 all_to_all.21
  731.1 71.3 %all-gather.10.cloned.1.call-done = bf16[512,3072]{1,0:T(8,128)(2,1)} async-done(((bf16[16,3072]{1,0:T(8,128)(2,1)}), bf16[512,3072]{1,0:T(8,128)(2,1)}) %all-gather.10.cloned.1.call-update) | async-done | bytes 3145744 | tf_op jit(solution)/shard_map/all_gather | solution.py:71
  802.5 3.1 fusion
  807.7 3.7 add_convert_fusion
  813.3 215.6 %reduce-scatter.5.cloned.1.call-done = bf16[16,3072]{1,0:T(8,128)(2,1)} async-done(((bf16[512,3072]{1,0:T(8,128)(2,1)}), bf16[16,3072]{1,0:T(8,128)(2,1)}) %reduce-scatter.5.cloned.1.call-update) | async-done | bytes 98320 | tf_op jit(solution)/shard_map/reduce_scatter | solution.py:76
  1030.5 10.2 all-to-all-start.3
  1040.7 4.9 all-to-all-done.3
  1047.0 3.2 multiply_convert_fusion
  1062.8 166.8 %all-gather.14.cloned.1.call-done = bf16[1536,64,64]{2,1,0:T(8,128)(2,1)} async-done(((bf16[48,64,64]{2,1,0:T(8,128)(2,1)}), bf16[1536,64,64]{2,1,0:T(8,128)(2,1)}) %all-gather.14.cloned.1.call-update) | async-done | bytes 12582928 | tf_op jit(solution)/shard_map/all_gather | solution.py:17
  1229.8 68.8 %while.27 = (s32[]{:T(128)}, f32[48,64,64]{2,1,0:T(8,128)S(1)}, s32[]{:T(128)}, bf16[32,48]{1,0:T(8,128)(2,1)}, bf16[32,48,64,64]{3,2,1,0:T(8,128)(2,1)}, /*index=5*/s32[]{:T(128)}, s32[]{:T(128)}, s32[]{:T(128)}, s32[]{:T(128)}) while((s32[]{:T(128)}, f32[48,64,64]{2,1,0:T(8,128)S(1)}, s32[]{:T(128)}, bf16[32,48]{1,0:T(8,128)(2,1)}, ...), condition=%wide.region_21.22_spmd, body=%wide.region_20.21_spmd.sunk | while | flops 589878 | bytes 1966715 | solution.py:32
  1298.6 2.4 fusion.13
  1302.2 4.1 fusion.11
  1306.3 2.3 copy.78
  (279 shorter events, 156.0 us)
Async XLA Ops:
  7.2 361.2 %copy-start = (bf16[1,288,3072]{2,1,0:T(8,128)(2,1)S(1)}, bf16[1,288,3072]{2,1,0:T(8,128)(2,1)}, u32[]{:S(2)}) copy-start(bf16[1,288,3072]{2,1,0:T(8,128)(2,1)} %param.33) | copy-start | bytes 5308420
  7.2 194.1 %all-gather.12.cloned.1.call-start = ((), (), s32[]{:S(2)}) async-start(), calls=%async_computation.10 | async-start | bytes 25952256 | tf_op jit(solution)/shard_map/all_gather | solution.py:17
  8.4 77.3 %copy-start.24 = (f32[48,128]{1,0:T(8,128)}, f32[48,128]{1,0:T(8,128)S(1)}, u32[]{:S(2)}) copy-start(f32[48,128]{1,0:T(8,128)S(1)} %reduce_window_sum.22) | copy-start | bytes 73732
  10.2 75.5 %copy-start.2 = (bf16[1,128,3072]{1,2,0:T(8,128)(2,1)}, bf16[1,128,3072]{1,2,0:T(8,128)(2,1)S(1)}, u32[]{:S(2)}) copy-start(bf16[1,128,3072]{1,2,0:T(8,128)(2,1)S(1)} %copy.58) | copy-start | bytes 2359300
  12.0 74.8 %copy-start.4 = (bf16[1,128,3072]{1,2,0:T(8,128)(2,1)}, bf16[1,128,3072]{1,2,0:T(8,128)(2,1)S(1)}, u32[]{:S(2)}) copy-start(bf16[1,128,3072]{1,2,0:T(8,128)(2,1)S(1)} %copy.60) | copy-start | bytes 2359300
  12.0 70.9 %copy-start.49 = (s32[1,4]{1,0:T(1,128)S(1)}, s32[1,4]{1,0:T(1,128)}, u32[]{:S(2)}) copy-start(s32[1,4]{1,0:T(1,128)} %param.24) | copy-start | bytes 52
  12.1 72.5 %copy-start.36 = (bf16[1,4,3072]{2,1,0:T(4,128)(2,1)S(1)}, bf16[1,4,3072]{2,1,0:T(4,128)(2,1)}, u32[]{:S(2)}) copy-start(bf16[1,4,3072]{2,1,0:T(4,128)(2,1)} %param.20) | copy-start | bytes 73732
  12.1 72.6 %copy-start.25 = (bf16[1,4,3072]{2,1,0:T(4,128)(2,1)S(1)}, bf16[1,4,3072]{2,1,0:T(4,128)(2,1)}, u32[]{:S(2)}) copy-start(bf16[1,4,3072]{2,1,0:T(4,128)(2,1)} %param.19) | copy-start | bytes 73732
  14.3 348.2 %all-gather.8.cloned.1.call-start = ((), (), s32[]{:S(2)}) async-start(), calls=%async_computation.6 | async-start | bytes 3244032 | tf_op jit(solution)/shard_map/all_gather | solution.py:71
  84.7 116.8 %copy-start.12 = (bf16[4,48,64]{2,1,0:T(8,128)(2,1)}, bf16[4,48,64]{2,1,0:T(8,128)(2,1)S(1)}, u32[]{:S(2)}) copy-start(bf16[4,48,64]{2,1,0:T(8,128)(2,1)S(1)} %reshape_squeeze.9) | copy-start | bytes 73732
  85.7 115.8 %copy-start.52 = (pred[4,128]{1,0:T(4,128)(4,1)}, pred[4,128]{1,0:T(4,128)(4,1)S(1)}, u32[]{:S(2)}) copy-start(pred[4,128]{1,0:T(4,128)(4,1)S(1)} %iota_compare_fusion.6) | copy-start | bytes 1540
  225.2 364.4 %reduce-scatter.3.cloned.1.call-start = ((), (), s32[]{:S(2)}) async-start(), calls=%async_computation.7 | async-start | bytes 3244032 | tf_op jit(solution)/shard_map/reduce_scatter | solution.py:76
  591.1 14.7 %all-to-all-start.1 = ((bf16[8,2,3072]{2,1,0:T(2,128)(2,1)}), bf16[8,2,3072]{2,1,0:T(2,128)(2,1)}, u32[]{:S(2)}, u32[]{:S(2)}) async-start(bf16[8,2,3072]{2,1,0:T(2,128)(2,1)} %reshape.392), calls=%async_computation.2 | async-start | bytes 196608 | tf_op jit(solution)/shard_map/all_to_all | solution.py:83
  600.8 201.7 %all-gather.10.cloned.1.call-start = ((), (), s32[]{:S(2)}) async-start(), calls=%async_computation.8 | async-start | bytes 3244032 | tf_op jit(solution)/shard_map/all_gather | solution.py:71
  730.9 298.0 %reduce-scatter.5.cloned.1.call-start = ((), (), s32[]{:S(2)}) async-start(), calls=%async_computation.9 | async-start | bytes 3244032 | tf_op jit(solution)/shard_map/reduce_scatter | solution.py:76
  811.4 229.2 %copy-start.45 = (f32[4,1]{0,1:T(1,128)S(1)}, f32[4,1]{0,1:T(1,128)}, u32[]{:S(2)}) copy-start(f32[4,1]{0,1:T(1,128)} %get-tuple-element.175) | copy-start | bytes 52
  811.4 234.3 %copy-start.39 = (bf16[4,2,16]{2,0,1:T(4,128)(2,1)S(1)}, bf16[4,2,16]{2,0,1:T(4,128)(2,1)}, u32[]{:S(2)}) copy-start(bf16[4,2,16]{2,0,1:T(4,128)(2,1)} %copy.67) | copy-start | bytes 772
  811.4 234.5 %copy-start.18 = (f32[4,3072]{1,0:T(4,128)S(1)}, f32[4,3072]{1,0:T(4,128)}, u32[]{:S(2)}) copy-start(f32[4,3072]{1,0:T(4,128)} %reshape.388) | copy-start | bytes 147460
  811.4 234.5 %copy-start.26 = (bf16[1,4,3072]{2,1,0:T(4,128)(2,1)S(1)}, bf16[1,4,3072]{2,1,0:T(4,128)(2,1)}, u32[]{:S(2)}) copy-start(bf16[1,4,3072]{2,1,0:T(4,128)(2,1)} %param.19) | copy-start | bytes 73732
  811.4 234.5 %copy-start.42 = (f32[4]{0:T(128)S(1)}, f32[4]{0:T(128)}, u32[]{:S(2)}) copy-start(f32[4]{0:T(128)} %add_rsqrt_fusion) | copy-start | bytes 52
  812.1 234.9 %copy-start.13 = (bf16[4,48,64]{2,1,0:T(8,128)(2,1)S(1)}, bf16[4,48,64]{2,1,0:T(8,128)(2,1)}, u32[]{:S(2)}) copy-start(bf16[4,48,64]{2,1,0:T(8,128)(2,1)} %copy-done.12) | copy-start | bytes 73732
  1030.5 15.1 %all-to-all-start.3 = ((bf16[8,2,3072]{2,1,0:T(2,128)(2,1)}), bf16[8,2,3072]{2,1,0:T(2,128)(2,1)S(1)}, u32[]{:S(2)}, u32[]{:S(2)}) async-start(bf16[8,2,3072]{2,1,0:T(2,128)(2,1)} %reshape.398), calls=%async_computation.5 | async-start | bytes 196608 | tf_op jit(solution)/shard_map/all_to_all | solution.py:83
  1040.6 189.0 %all-gather.14.cloned.1.call-start = ((), (), s32[]{:S(2)}) async-start(), calls=%async_computation.11 | async-start | bytes 25952256 | tf_op jit(solution)/shard_map/all_gather | solution.py:17
  1229.8 68.9 %copy-start.22 = (f32[128,48]{0,1:T(8,128)S(1)}, f32[128,48]{0,1:T(8,128)}, u32[]{:S(2)}) copy-start(f32[128,48]{0,1:T(8,128)} %copy-done.21) | copy-start | bytes 73732
  (37 other events, 112.2 us)
Sparse Core Ops, SparseCore 0:
  14.5 186.7 all-gather.11
  225.3 137.1 all-gather.7
  372.1 217.4 reduce-scatter.2
  731.0 71.3 all-gather.9
  811.6 217.2 reduce-scatter.4
  1050.3 179.2 all-gather.13
